TPU v7x, 32 devices: a whole 2x2x4 slice. The times are simulated.
32 devices in a mesh: dp: 16 (over z, y, core), tensor: 2 (over x).
Axes of the slice: x: 2, y: 2, z: 4, core: 2. Of those that a mesh axis runs over, the one named last changes fastest.
Arguments:
- tokens: bfloat16 [4096, 6144], P('dp', 'tensor'), may hold values from -6 to 6
- grad_out: bfloat16 [4096, 6144], P('dp', 'tensor'), may hold values from -6 to 6
- input_norm_gain: float32 [6144], replicated, may hold values from 0.1 to 1.9
- q_gain: float32 [128], replicated, may hold values from 0.1 to 1.9
- k_gain: float32 [128], replicated, may hold values from 0.1 to 1.9
- w_qkv: bfloat16 [3, 6144, 3072], P(None, 'dp', 'tensor'), may hold values from -0.078125 to 0.078125
- w_out: bfloat16 [3072, 6144], P('tensor', 'dp'), may hold values from -0.109375 to 0.109375
- pattern: int32 [24, 4, 2], P('tensor'), may hold values from 0 to 3, all different within a row
Outputs:
- tokens_grad: bfloat16 [4096, 6144], P('dp', 'tensor')
All inputs are finite; a program needn't handle non-finite values.
Results may differ from a plain program's by a relative error of at most 0.015.
Values may be sent and summed in bfloat16 or wider, within the bound.
A program may use at most 192 MiB of HBM per device.

v0:
```python
import math
import jax
import jax.numpy as jnp
from jax import lax
from jax.sharding import PartitionSpec as P

HD = 128
SEQ = 256
BLK = 64


def norm_rows(values, gain):
    centre = jnp.mean(values, axis=-1, keepdims=True)
    centered_input = values - centre
    inverse_deviation = lax.rsqrt(
        jnp.mean(centered_input * centered_input, axis=-1, keepdims=True) + 1e-06
    )
    return centered_input * inverse_deviation * gain


def block_mask(pattern, seq_len, block):
    count = seq_len // block
    hits = pattern[:, :, :, None] == jnp.arange(count, dtype=jnp.int32)[None, None, None, :]
    allowed = jnp.any(hits, axis=2).astype(jnp.float32)
    heads = allowed.shape[0]
    spread = jnp.broadcast_to(allowed[:, :, None, :, None], (heads, count, block, count, block))
    return spread.reshape(heads, seq_len, seq_len)


def attention_grads(stacked, upstream, q_gain, k_gain, allowed):

    def attend(query, key, value):
        q_normed = norm_rows(query, q_gain)
        k_normed = norm_rows(key, k_gain)
        scores = jnp.einsum(
            "aqhd,akhd->ahqk", q_normed, k_normed, precision=lax.Precision.HIGHEST
        ) / math.sqrt(query.shape[-1])
        weights = jnp.exp(scores) * allowed[None]
        probs = weights / jnp.sum(weights, axis=-1, keepdims=True)
        return jnp.einsum("ahqk,akhd->aqhd", probs, value, precision=lax.Precision.HIGHEST)

    widened = stacked.astype(jnp.float32)
    _, pull = jax.vjp(attend, widened[0], widened[1], widened[2])
    grads = pull(upstream.astype(jnp.float32))
    return jnp.stack(grads).astype(jnp.bfloat16)


def body(tokens, grad_out, input_norm_gain, q_gain, k_gain, w_qkv, w_out, pattern):
    width = tokens.shape[1]
    row_count = tokens.shape[0]
    rows_full, grads_full = (
        lax.all_gather(tokens, "tensor", axis=1, tiled=True),
        lax.all_gather(grad_out, "tensor", axis=1, tiled=True),
    )
    values = rows_full.astype(jnp.float32)
    centre = jnp.mean(values, axis=-1, keepdims=True)
    centered_input = values - centre
    inverse_deviation = lax.rsqrt(
        jnp.mean(centered_input * centered_input, axis=-1, keepdims=True) + 1e-06
    )
    standardized_input = centered_input * inverse_deviation
    normalized_input = (standardized_input * input_norm_gain).astype(jnp.bfloat16)
    whole = lax.all_gather(w_qkv, "dp", axis=1, tiled=True)
    qkv = jnp.einsum(
        "rd,idh->irh", normalized_input, whole, preferred_element_type=jnp.float32
    ).astype(jnp.bfloat16)
    local_width = whole.shape[2]
    upstream = lax.dot_general(
        grads_full,
        lax.all_gather(w_out, "dp", axis=1, tiled=True),
        (((1,), (1,)), ((), ())),
        preferred_element_type=jnp.float32,
    ).astype(jnp.bfloat16)
    local_heads = local_width // HD
    images = row_count // SEQ
    allowed = block_mask(pattern, SEQ, BLK)
    d_qkv = attention_grads(
        qkv.reshape(3, images, SEQ, local_heads, HD),
        upstream.reshape(images, SEQ, local_heads, HD),
        q_gain,
        k_gain,
        allowed,
    )
    d_qkv = d_qkv.reshape(3, row_count, local_width)
    partial_grad = jnp.einsum("irh,idh->rd", d_qkv, whole, preferred_element_type=jnp.float32)
    offset = lax.axis_index("tensor") * width
    d_normed = lax.psum(partial_grad.astype(jnp.bfloat16), "tensor").astype(jnp.float32)
    normalized_gradient = d_normed * input_norm_gain
    leading_term = jnp.mean(normalized_gradient, axis=-1, keepdims=True)
    trailing_term = jnp.mean(normalized_gradient * standardized_input, axis=-1, keepdims=True)
    complete_gradient = inverse_deviation * (
        normalized_gradient - leading_term - standardized_input * trailing_term
    )
    result = lax.dynamic_slice_in_dim(complete_gradient, offset, width, 1)
    return result.astype(jnp.bfloat16)


def solution(mesh):
    return jax.shard_map(
        body,
        mesh=mesh,
        in_specs=(
            P("dp", "tensor"),
            P("dp", "tensor"),
            P(),
            P(),
            P(),
            P(None, "dp", "tensor"),
            P("tensor", "dp"),
            P("tensor", None, None),
        ),
        out_specs=P("dp", "tensor"),
        check_vma=False,
    )
```

profile of v0, /device:TPU:0, one launch (start us, length us, event | category | flops | bytes accessed | tf_op | source)
XLA Modules:
  0.0 674.1 jit_solution(7555071908021062251)
XLA Ops:
  6.5 0.7 all-gather.5.cloned.1.call-update
  7.3 0.0 all-gather.7.cloned.1.call-start
  7.3 0.7 all-gather.7.cloned.1.call-update
  8.0 0.0 all-gather.9.cloned.1.call-start
  8.1 0.7 all-gather.9.cloned.1.call-update
  8.8 0.5 all-gather.11.cloned.1.call-update
  9.3 0.0 all-reduce.2.cloned.1.call-start
  9.4 0.1 copy.49
  9.5 3.6 broadcast_in_dim.14
  13.2 7.0 %broadcast_in_dim_reshape.3 = f32[12,256,256]{1,2,0:T(8,128)} reshape(f32[12,4,64,4,64]{2,1,4,3,0:T(4,128)} %broadcast_in_dim.14) | data formatting | bytes 6291456 | tf_op jit(solution)/shard_map/jvp()/broadcast_in_dim;reshape | solution.py:38
  20.2 36.4 %all-gather.5.cloned.1.call-done = bf16[256,6144]{1,0:T(8,128)(2,1)} async-done(((bf16[256,3072]{1,0:T(8,128)(2,1)}), bf16[256,6144]{1,0:T(8,128)(2,1)}) %all-gather.5.cloned.1.call-update) | async-done | bytes 3145744 | tf_op jit(solution)/shard_map/all_gather | solution.py:52
  56.6 2.5 convert_reduce_fusion
  59.1 0.3 copy-done.3
  59.4 1.0 fusion.3
  60.4 42.7 %all-gather.7.cloned.1.call-done = bf16[256,6144]{1,0:T(8,128)(2,1)} async-done(((bf16[256,3072]{1,0:T(8,128)(2,1)}), bf16[256,6144]{1,0:T(8,128)(2,1)}) %all-gather.7.cloned.1.call-update) | async-done | bytes 3145744 | tf_op jit(solution)/shard_map/all_gather | solution.py:53
  103.1 100.4 %all-gather.9.cloned.1.call-done = bf16[1536,6144]{1,0:T(8,128)(2,1)} async-done(((bf16[1536,384]{1,0:T(8,128)(2,1)}), bf16[1536,6144]{1,0:T(8,128)(2,1)}) %all-gather.9.cloned.1.call-update) | async-done | bytes 18874384 | tf_op jit(solution)/shard_map/all_gather | solution.py:70
  203.5 10.6 %convolution_convert_fusion.1 = bf16[256,1536]{1,0:T(8,128)(2,1)} fusion(bf16[256,6144]{1,0:T(8,128)(2,1)} %all-gather.7.cloned.1.call-done, bf16[1536,6144]{1,0:T(8,128)(2,1)} %all-gather.9.cloned.1.call-done), kind=kOutput, calls=%fused_computation.25 | convolution fusion | flops 4832231424 | bytes 22806528 | tf_op jit(solution)/shard_map/dot_general | solution.py:68
  214.1 2.4 copy.40
  216.5 265.2 %all-gather.11.cloned.1.call-done = bf16[3,6144,1536]{2,1,0:T(8,128)(2,1)} async-done(((bf16[3,384,1536]{2,1,0:T(8,128)(2,1)}), bf16[3,6144,1536]{2,1,0:T(8,128)(2,1)}) %all-gather.11.cloned.1.call-update) | async-done | bytes 56623120 | tf_op jit(solution)/shard_map/all_gather | solution.py:63
  481.7 24.1 %fusion.12 = bf16[3,256,1536]{2,1,0:T(8,128)(2,1)} fusion(bf16[3,6144,1536]{2,1,0:T(8,128)(2,1)} %all-gather.11.cloned.1.call-done, f32[6144]{0:T(1024)S(1)} %copy-done.9, bf16[256,6144]{1,0:T(8,128)(2,1)S(1)} %copy-done.3, f32[256]{0:T(256)S(1)} %add_rsqrt_fusion, f32[256]{0:T(256)S(1)} %broadcast_multiply_fusion.4), kind=kOutput, calls=%fused_computation.23 | convolution fusion | flops 14504558592 | bytes 62154752 | tf_op jit(solution)/shard_map/rd,idh->irh/dot_general | solution.py:64
  505.8 2.9 fusion.50
  508.7 2.1 slice.15
  510.8 0.5 copy.45
  511.2 1.9 copy.43
  513.1 0.1 reduce_sum.126
  513.3 0.1 reduce_sum.128
  513.4 0.2 multiply_reduce_fusion.3
  513.6 0.2 multiply_reduce_fusion.2
  513.8 0.1 copy-done.10
  513.9 1.4 copy-done
  515.3 5.4 fusion.48
  520.7 2.3 copy.41
  523.0 6.4 fusion.25
  529.5 1.0 multiply_reduce_fusion.1
  530.5 0.9 multiply_multiply_fusion
  531.4 5.0 fusion.22
  536.5 3.5 fusion.23
  540.0 2.3 copy.55
  542.3 1.9 fusion.42
  544.3 1.4 add_convert_fusion
  545.6 2.4 copy.54
  548.1 0.4 fusion.41
  548.5 1.3 add_convert_fusion.1
  549.8 1.4 copy.53
  551.2 24.2 %fusion = bf16[256,6144]{1,0:T(8,128)(2,1)} fusion(bf16[3,6144,1536]{2,1,0:T(8,128)(2,1)} %all-gather.11.cloned.1.call-done, bf16[1,256,1536]{2,1,0:T(8,128)(2,1)} %copy.55, bf16[1,256,1536]{2,1,0:T(8,128)(2,1)} %copy.54, bf16[1,256,1536]{2,1,0:T(8,128)(2,1)S(1)} %copy.53), kind=kOutput, calls=%fused_computation.3 | convolution fusion | flops 14499446784 | bytes 62128128 | tf_op jit(solution)/shard_map/irh,idh->rd/dot_general | solution.py:85
  575.4 85.8 %all-reduce.2.cloned.1.call-done = bf16[256,6144]{1,0:T(8,128)(2,1)} async-done(((bf16[256,6144]{1,0:T(8,128)(2,1)}), bf16[256,6144]{1,0:T(8,128)(2,1)}) %all-reduce.2.cloned.1.call-update) | async-done | bytes 3145744 | tf_op jit(solution)/shard_map/psum | solution.py:87
  661.3 4.1 fusion.16
  665.4 2.2 fusion.8
  (41 shorter events, 0.2 us)
Async XLA Ops:
  6.5 50.0 %all-gather.5.cloned.1.call-start = ((), (), s32[]{:S(2)}) async-start(), calls=%async_computation | async-start | bytes 4718592 | tf_op jit(solution)/shard_map/all_gather | solution.py:52
  7.3 95.8 %all-gather.7.cloned.1.call-start = ((), (), s32[]{:S(2)}) async-start(), calls=%async_computation.1 | async-start | bytes 4718592 | tf_op jit(solution)/shard_map/all_gather | solution.py:53
  8.0 1.4 copy-start.12
  8.0 195.5 %all-gather.9.cloned.1.call-start = ((), (), s32[]{:S(2)}) async-start(), calls=%async_computation.2 | async-start | bytes 20054016 | tf_op jit(solution)/shard_map/all_gather | solution.py:70
  8.8 472.9 %all-gather.11.cloned.1.call-start = ((), (), s32[]{:S(2)}) async-start(), calls=%async_computation.3 | async-start | bytes 60162048 | tf_op jit(solution)/shard_map/all_gather | solution.py:63
  9.3 651.9 %all-reduce.2.cloned.1.call-start = ((), (), s32[]{:S(2)}) async-start(), calls=%async_computation.4 | async-start | bytes 6291456 | tf_op jit(solution)/shard_map/psum | solution.py:87
  56.6 2.8 copy-start.3
  60.4 421.3 %copy-start.9 = (f32[6144]{0:T(1024)S(1)}, f32[6144]{0:T(1024)}, u32[]{:S(2)}) copy-start(f32[6144]{0:T(1024)} %param.10) | copy-start | bytes 73732
  513.3 0.7 copy-start.10
  513.3 0.7 copy-start.11
  513.4 1.9 copy-start
  523.0 6.5 copy-start.1
  523.0 6.5 copy-start.2
  523.0 6.5 copy-start.7
  523.0 6.5 copy-start.8
  542.3 2.0 copy-start.6
  545.6 2.4 copy-start.5
  575.4 85.9 %copy-start.4 = (bf16[256,6144]{1,0:T(8,128)(2,1)S(1)}, bf16[256,6144]{1,0:T(8,128)(2,1)}, u32[]{:S(2)}) copy-start(bf16[256,6144]{1,0:T(8,128)(2,1)} %all-gather.5.cloned.1.call-done) | copy-start | bytes 9437188
Sparse Core Ops, SparseCore 0:
  8.9 47.6 all-gather.4
  58.1 44.9 all-gather.6
  104.6 98.8 all-gather.8
  204.9 276.7 all-gather.10
  575.5 85.6 all-reduce.1
where the time goes:
time: 675 us; the launch traced here: 674 us
  waiting for transfers between devices  533 us (79%)
  matrix products  80.3 us (12%)
  local copies, waits for them, and re-layouts  30.7 us (5%)
  other arithmetic  16.4 us (2%)
  between operations  13.4 us (2%)
    all_gather x1, waiting for transfers between devices, body(): whole = lax.all_gather(w_qkv, 'dp', axis=1, tiled=True)  265 us
    all_gather x1, waiting for transfers between devices, body(): lax.all_gather(w_out, 'dp', axis=1, tiled=True)  100 us
    psum x1, waiting for transfers between devices, body(): lax.psum(partial_grad.astype(jnp.bfloat16), 'tensor').astype(jnp.float32)  85.8 us
    all_gather x1, waiting for transfers between devices, body(): lax.all_gather(grad_out, 'tensor', axis=1, tiled=True)  42.7 us
    all_gather x1, waiting for transfers between devices, body(): lax.all_gather(tokens, 'tensor', axis=1, tiled=True)  36.4 us
    dot_general x1, matrix products, body(): jnp.einsum('irh,idh->rd', d_qkv, whole, preferred_element_type=jnp.float32)  24.2 us
    dot_general x1, matrix products, body(): jnp.einsum('rd,idh->irh', normalized_input, whole, preferred_element_type...  24.1 us
    dot_general x3, matrix products, attend(): jnp.einsum('aqhd,akhd->ahqk', q_normed, k_normed, precision=lax.Precision...  14 us
  transfers between devices with their start and end apart: 5, of which 5 were waited for; matrix products, arithmetic and copies ran while one was open for 4% of the time, Pallas kernels for 0%

commit v1 on v0

--- a/solution.py
+++ b/solution.py
@@ -50,7 +50,9 @@
     row_count = tokens.shape[0]
     rows_full, grads_full = (
         lax.all_gather(tokens, "tensor", axis=1, tiled=True),
-        lax.all_gather(grad_out, "tensor", axis=1, tiled=True),
+        jnp.concatenate(
+            lax.all_to_all(jnp.stack([grad_out] * lax.axis_size("tensor")), "tensor", 0, 0), axis=1
+        ),
     )
     values = rows_full.astype(jnp.float32)
     centre = jnp.mean(values, axis=-1, keepdims=True)

time: 675 us -> 661 us (0.979)
  waiting for transfers between devices: 533 us -> 511 us
    all_gather x1 -> x0, waiting for transfers between devices: 42.7 us -> none  [body(): lax.all_gather(grad_out, 'tensor', axis=1, tiled=True)]
    all_gather x1, waiting for transfers between devices: 36.4 us -> 60.5 us  [body(): lax.all_gather(tokens, 'tensor', axis=1, tiled=True)]
  transfers between devices with their start and end apart: 5 -> 5, of which waited for: 5 -> 4; matrix products, arithmetic and copies ran while one was open for 4% -> 5% of each run, Pallas kernels for 0% -> 0%
where the time goes in v1:
time: 661 us; the launch traced here: 660 us
  waiting for transfers between devices  511 us (77%)
  matrix products  80.4 us (12%)
  local copies, waits for them, and re-layouts  31.5 us (5%)
  other arithmetic  18.4 us (3%)
  between operations  13.4 us (2%)
    all_gather x1, waiting for transfers between devices, body(): whole = lax.all_gather(w_qkv, 'dp', axis=1, tiled=True)  265 us
    all_gather x1, waiting for transfers between devices, body(): lax.all_gather(w_out, 'dp', axis=1, tiled=True)  97.2 us
    psum x1, waiting for transfers between devices, body(): lax.psum(partial_grad.astype(jnp.bfloat16), 'tensor').astype(jnp.float32)  85.9 us
    all_gather x1, waiting for transfers between devices, body(): lax.all_gather(tokens, 'tensor', axis=1, tiled=True)  60.5 us
    dot_general x1, matrix products, body(): jnp.einsum('irh,idh->rd', d_qkv, whole, preferred_element_type=jnp.float32)  24.2 us
    dot_general x1, matrix products, body(): jnp.einsum('rd,idh->irh', normalized_input, whole, preferred_element_type...  24.1 us
    dot_general x3, matrix products, attend(): jnp.einsum('aqhd,akhd->ahqk', q_normed, k_normed, precision=lax.Precision...  14 us
  transfers between devices with their start and end apart: 5, of which 4 were waited for; matrix products, arithmetic and copies ran while one was open for 5% of the time, Pallas kernels for 0%

profile of v1, /device:TPU:0, one launch (start us, length us, event | category | flops | bytes accessed | tf_op | source)
XLA Modules:
  0.0 660.0 jit_solution(11699399383068684348)
XLA Ops:
  6.5 0.7 all-gather.4.cloned.1.call-update
  7.3 0.0 all-gather.6.cloned.1.call-start
  7.3 0.7 all-gather.6.cloned.1.call-update
  8.1 0.7 all-gather.8.cloned.1.call-update
  8.8 0.7 copy.41
  9.5 2.0 pad_maximum_fusion
  11.4 5.3 all-to-all-start
  16.8 0.0 all-reduce.2.cloned.1.call-start
  16.9 0.1 copy.51
  17.0 3.7 broadcast_in_dim.14
  20.7 7.0 %broadcast_in_dim_reshape.3 = f32[12,256,256]{1,2,0:T(8,128)} reshape(f32[12,4,64,4,64]{2,1,4,3,0:T(4,128)} %broadcast_in_dim.14) | data formatting | bytes 6291456 | tf_op jit(solution)/shard_map/jvp()/broadcast_in_dim;reshape | solution.py:38
  27.7 60.5 %all-gather.4.cloned.1.call-done = bf16[256,6144]{1,0:T(8,128)(2,1)} async-done(((bf16[256,3072]{1,0:T(8,128)(2,1)}), bf16[256,6144]{1,0:T(8,128)(2,1)}) %all-gather.4.cloned.1.call-update) | async-done | bytes 3145744 | tf_op jit(solution)/shard_map/all_gather | solution.py:52
  88.2 2.5 convert_reduce_fusion
  90.8 0.3 copy-done.3
  91.1 1.0 fusion.3
  92.1 97.2 %all-gather.6.cloned.1.call-done = bf16[1536,6144]{1,0:T(8,128)(2,1)} async-done(((bf16[1536,384]{1,0:T(8,128)(2,1)}), bf16[1536,6144]{1,0:T(8,128)(2,1)}) %all-gather.6.cloned.1.call-update) | async-done | bytes 18874384 | tf_op jit(solution)/shard_map/all_gather | solution.py:72
  189.2 10.7 %convolution_convert_fusion.1 = bf16[256,1536]{1,0:T(8,128)(2,1)} fusion(bf16[256,6144]{0,1:T(8,128)(2,1)} %bitcast.2, bf16[1536,6144]{1,0:T(8,128)(2,1)} %all-gather.6.cloned.1.call-done), kind=kOutput, calls=%fused_computation.26 | convolution fusion | flops 4832231424 | bytes 22806528 | tf_op jit(solution)/shard_map/dot_general | solution.py:70
  199.9 2.4 copy.42
  202.3 265.2 %all-gather.8.cloned.1.call-done = bf16[3,6144,1536]{2,1,0:T(8,128)(2,1)} async-done(((bf16[3,384,1536]{2,1,0:T(8,128)(2,1)}), bf16[3,6144,1536]{2,1,0:T(8,128)(2,1)}) %all-gather.8.cloned.1.call-update) | async-done | bytes 56623120 | tf_op jit(solution)/shard_map/all_gather | solution.py:65
  467.5 24.1 %fusion.12 = bf16[3,256,1536]{2,1,0:T(8,128)(2,1)} fusion(bf16[3,6144,1536]{2,1,0:T(8,128)(2,1)} %all-gather.8.cloned.1.call-done, f32[6144]{0:T(1024)S(1)} %copy-done.10, bf16[256,6144]{1,0:T(8,128)(2,1)S(1)} %copy-done.3, f32[256]{0:T(256)S(1)} %add_rsqrt_fusion, f32[256]{0:T(256)S(1)} %broadcast_multiply_fusion.4), kind=kOutput, calls=%fused_computation.24 | convolution fusion | flops 14504558592 | bytes 62154752 | tf_op jit(solution)/shard_map/rd,idh->irh/dot_general | solution.py:66
  491.6 2.9 fusion.50
  494.5 2.1 slice.15
  496.6 0.5 copy.47
  497.1 1.9 copy.45
  499.0 0.1 reduce_sum.126
  499.1 0.1 reduce_sum.128
  499.3 0.2 multiply_reduce_fusion.3
  499.5 0.2 multiply_reduce_fusion.2
  499.7 0.1 copy-done.11
  499.8 1.4 copy-done
  501.1 5.4 fusion.48
  506.6 2.3 copy.43
  508.9 6.4 fusion.25
  515.3 1.0 multiply_reduce_fusion.1
  516.3 0.9 multiply_multiply_fusion
  517.3 5.0 fusion.22
  522.3 3.5 fusion.23
  525.8 2.3 copy.57
  528.2 1.9 fusion.42
  530.1 1.4 add_convert_fusion
  531.5 2.4 copy.56
  533.9 0.4 fusion.41
  534.3 1.3 add_convert_fusion.1
  535.6 1.4 copy.55
  537.0 24.2 %fusion = bf16[256,6144]{1,0:T(8,128)(2,1)} fusion(bf16[3,6144,1536]{2,1,0:T(8,128)(2,1)} %all-gather.8.cloned.1.call-done, bf16[1,256,1536]{2,1,0:T(8,128)(2,1)} %copy.57, bf16[1,256,1536]{2,1,0:T(8,128)(2,1)} %copy.56, bf16[1,256,1536]{2,1,0:T(8,128)(2,1)S(1)} %copy.55), kind=kOutput, calls=%fused_computation.3 | convolution fusion | flops 14499446784 | bytes 62128128 | tf_op jit(solution)/shard_map/irh,idh->rd/dot_general | solution.py:87
  561.3 85.9 %all-reduce.2.cloned.1.call-done = bf16[256,6144]{1,0:T(8,128)(2,1)} async-done(((bf16[256,6144]{1,0:T(8,128)(2,1)}), bf16[256,6144]{1,0:T(8,128)(2,1)}) %all-reduce.2.cloned.1.call-update) | async-done | bytes 3145744 | tf_op jit(solution)/shard_map/psum | solution.py:89
  647.2 4.1 fusion.16
  651.3 2.2 fusion.8
  (44 shorter events, 0.3 us)
Async XLA Ops:
  6.5 81.7 %all-gather.4.cloned.1.call-start = ((), (), s32[]{:S(2)}) async-start(), calls=%async_computation.1 | async-start | bytes 4718592 | tf_op jit(solution)/shard_map/all_gather | solution.py:52
  7.3 1.5 copy-start.9
  7.3 182.0 %all-gather.6.cloned.1.call-start = ((), (), s32[]{:S(2)}) async-start(), calls=%async_computation.2 | async-start | bytes 20054016 | tf_op jit(solution)/shard_map/all_gather | solution.py:72
  8.0 459.5 %all-gather.8.cloned.1.call-start = ((), (), s32[]{:S(2)}) async-start(), calls=%async_computation.3 | async-start | bytes 60162048 | tf_op jit(solution)/shard_map/all_gather | solution.py:65
  11.4 5.4 copy-start.13
  11.4 80.6 %all-to-all-start = ((bf16[2,256,3072]{1,2,0:T(8,128)(2,1)}), bf16[2,256,3072]{1,2,0:T(8,128)(2,1)}, u32[]{:S(2)}, u32[]{:S(2)}) async-start(bf16[2,256,3072]{1,2,0:T(8,128)(2,1)} %pad_maximum_fusion), calls=%async_computation | async-start | bytes 6291456 | tf_op jit(solution)/shard_map/all_to_all | solution.py:54
  16.8 630.4 %all-reduce.2.cloned.1.call-start = ((), (), s32[]{:S(2)}) async-start(), calls=%async_computation.4 | async-start | bytes 6291456 | tf_op jit(solution)/shard_map/psum | solution.py:89
  88.2 2.8 copy-start.3
  189.2 278.3 %copy-start.10 = (f32[6144]{0:T(1024)S(1)}, f32[6144]{0:T(1024)}, u32[]{:S(2)}) copy-start(f32[6144]{0:T(1024)} %param.10) | copy-start | bytes 73732
  499.1 0.7 copy-start.11
  499.1 0.7 copy-start.12
  499.2 1.9 copy-start
  508.8 6.5 copy-start.1
  508.9 6.5 copy-start.2
  508.9 6.5 copy-start.7
  508.9 6.5 copy-start.8
  528.1 2.0 copy-start.6
  531.5 2.4 copy-start.5
  561.2 85.9 %copy-start.4 = (bf16[256,6144]{1,0:T(8,128)(2,1)S(1)}, bf16[256,6144]{1,0:T(8,128)(2,1)}, u32[]{:S(2)}) copy-start(bf16[256,6144]{1,0:T(8,128)(2,1)} %all-gather.4.cloned.1.call-done) | copy-start | bytes 9437188
Sparse Core Ops, SparseCore 0:
  8.9 79.2 all-gather.3
  89.8 99.3 all-gather.5
  190.8 276.6 all-gather.7
  561.4 85.7 all-reduce.1
